TPU v7x, 32 devices: a whole 2x2x4 slice. The times are simulated.
32 devices in a mesh: outer: 4 (over y, x), inner: 8 (over z, core).
Axes of the slice: x: 2, y: 2, z: 4, core: 2. Of those that a mesh axis runs over, the one named last changes fastest.
Arguments:
- queries: bfloat16 [4096, 2048], P(('outer', 'inner')), may hold values from -6 to 6
- key_rows: bfloat16 [4096, 2048], P(('outer', 'inner')), may hold values from -6 to 6
- value_rows: bfloat16 [4096, 2048], P(('outer', 'inner')), may hold values from -6 to 6
- beta_logit: bfloat16 [4096, 16], P(('outer', 'inner')), may hold values from -8 to 2, as said below
- log_gate: bfloat16 [4096, 16], P(('outer', 'inner')), may hold values from -1 to 0, as said below
- out_grad: bfloat16 [4096, 2048], P(('outer', 'inner')), may hold values from -6 to 6
- block_states: float32 [4, 16, 128, 128], P('outer', 'inner'), may hold values from -4 to 4
Outputs:
- query_gradient: bfloat16 [4096, 2048], P(('outer', 'inner'))
- grad_keys: bfloat16 [4096, 2048], P(('outer', 'inner'))
- grad_values: bfloat16 [4096, 2048], P(('outer', 'inner'))
- grad_beta: bfloat16 [4096, 16], P(('outer', 'inner'))
- grad_gate: bfloat16 [4096, 16], P(('outer', 'inner'))
Inputs may be any that keep to these rules, and one draw needn't show every extreme that they name: `beta_logit`: within each head the logits lie within 1 of a level drawn for each head. `log_gate`: negative in every entry.
All inputs are finite; a program needn't handle non-finite values.
Results may differ from a plain program's by a relative error of at most 0.002.
Values may be sent and summed in bfloat16 or wider, within the bound.
A program may use at most 128 MiB of HBM per device.

v0:
```python
import jax
import jax.numpy as jnp
from jax import lax
from jax.sharding import PartitionSpec as P

DK = 128
DV = 128
GROUP = 128
precise = lax.Precision.HIGHEST


def unit_rows(matrix):
    return matrix * lax.rsqrt(jnp.sum(matrix * matrix, axis=-1, keepdims=True) + 1e-06)


def group_step(carried, inputs):
    state_now, transition, grad_sum = carried
    query_part, key_part, value_part, strength, gate_part, cotangent_part = inputs
    group_len = query_part.shape[1]
    key_width = key_part.shape[2]
    row_index = jnp.arange(group_len)[:, None]
    col_index = jnp.arange(group_len)[None, :]
    inclusive = row_index >= col_index
    strictly_lower = row_index > col_index
    cumulative = jnp.cumsum(gate_part, axis=1)
    gaps = cumulative[:, :, None] - cumulative[:, None, :]
    decay_mat = jnp.where(inclusive, jnp.exp(jnp.where(inclusive, gaps, 0.0)), 0.0)
    key_gram = jnp.einsum("hid,hjd->hij", key_part, key_part, precision=precise)
    lower_mat = strength[:, :, None] * jnp.where(strictly_lower, decay_mat, 0.0) * key_gram
    unit_lower = lower_mat + jnp.eye(group_len, dtype=jnp.float32)
    growth = jnp.exp(cumulative)
    right_side = jnp.concatenate(
        [(strength * growth)[:, :, None] * key_part, strength[:, :, None] * value_part], axis=2
    )
    solution_matrix = lax.linalg.triangular_solve(
        unit_lower, right_side, left_side=True, lower=True, unit_diagonal=True
    )
    write_keys = solution_matrix[:, :, :key_width]
    write_values = solution_matrix[:, :, key_width:]
    new_values = write_values - jnp.einsum("hcd,hde->hce", write_keys, state_now, precision=precise)
    scores = jnp.einsum("hid,hjd->hij", query_part, key_part, precision=precise) * decay_mat
    grown_queries = query_part * growth[:, :, None]
    output = jnp.einsum("hcd,hde->hce", grown_queries, state_now, precision=precise)
    output = output + jnp.einsum("hij,hje->hie", scores, new_values, precision=precise)
    tail_decay = jnp.exp(cumulative[:, -1:] - cumulative)
    tail_keys = key_part * tail_decay[:, :, None]
    last_growth = growth[:, -1][:, None, None]
    state_next = last_growth * state_now + jnp.einsum(
        "hcd,hce->hde", tail_keys, new_values, precision=precise
    )
    detached = lax.stop_gradient
    state_queries = detached(
        grown_queries - jnp.einsum("hij,hjd->hid", scores, write_keys, precision=precise)
    )
    projected = jnp.einsum("hcd,hce->hde", state_queries, cotangent_part, precision=precise)
    grad_sum = grad_sum + jnp.einsum("hji,hje->hie", transition, projected, precision=precise)
    step_trans = detached(
        last_growth * jnp.eye(key_width, dtype=jnp.float32)
        - jnp.einsum("hcd,hce->hde", tail_keys, write_keys, precision=precise)
    )
    transition = jnp.einsum("hij,hjk->hik", step_trans, transition, precision=precise)
    return ((state_next, transition, grad_sum), output)


def block_forward(queries, keys_in, values, logits, gates, start_state, cotangent, group_size):
    head_count, length, key_width = queries.shape
    group_count = length // group_size

    def to_groups(array_in):
        shaped = array_in.reshape((head_count, group_count, group_size) + array_in.shape[2:])
        return jnp.moveaxis(shaped, 1, 0)

    inputs = (
        to_groups(unit_rows(queries)),
        to_groups(unit_rows(keys_in)),
        to_groups(values),
        to_groups(jax.nn.sigmoid(logits)),
        to_groups(gates),
        to_groups(cotangent),
    )
    identity = jnp.broadcast_to(
        jnp.eye(key_width, dtype=jnp.float32), (head_count, key_width, key_width)
    )
    grad_zero = jnp.zeros(start_state.shape, jnp.float32)
    (final_state, transition, grad_sum), outputs = lax.scan(
        group_step, (start_state, identity, grad_zero), inputs
    )
    outputs = jnp.moveaxis(outputs, 0, 1).reshape(head_count, length, -1)
    return ((outputs, final_state), (transition, grad_sum))


def matmul_heads(left_mat, right_mat):
    return jnp.einsum("hij,hjk->hik", left_mat, right_mat, precision=precise)


def head_split(array_in, width):
    return array_in.astype(jnp.float32).reshape(array_in.shape[0], -1, width).transpose(1, 0, 2)


def merge_heads(array_in):
    return array_in.transpose(1, 0, 2).reshape(array_in.shape[1], -1).astype(jnp.bfloat16)


def prepare(queries, key_rows, value_rows, out_grad, beta_logit, log_gate):
    return (
        head_split(queries, DK),
        head_split(key_rows, DK),
        head_split(value_rows, DV),
        beta_logit.astype(jnp.float32).T,
        log_gate.astype(jnp.float32).T,
        head_split(out_grad, DV),
    )


def block_pullback(pieces, start_state):
    query_in, key_in, value_in, logit_in, gate_in, cotangent = pieces

    def forward(query_arg, key_arg, value_arg, logit_arg, gate_arg, state_arg):
        return block_forward(
            query_arg, key_arg, value_arg, logit_arg, gate_arg, state_arg, cotangent, GROUP
        )

    unused_out, pull_back, side = jax.vjp(
        forward, query_in, key_in, value_in, logit_in, gate_in, start_state, has_aux=True
    )
    turned = jnp.swapaxes(side[0], 1, 2)

    def finish(incoming):
        gradients = pull_back((cotangent, incoming))
        return gradients[:5]

    return (turned, side[1], finish)


def fold_later(matrices, state_grads, position):
    total_blocks = matrices.shape[0]

    def advance(turn_index, running):
        block_index = total_blocks - 1 - turn_index
        updated = matmul_heads(matrices[block_index], running) + state_grads[block_index]
        return jnp.where(block_index > position, updated, running)

    return lax.fori_loop(0, total_blocks, advance, jnp.zeros_like(state_grads[0]))


def shards(queries, key_rows, value_rows, beta_logit, log_gate, out_grad, block_states):
    arrived = (
        lax.all_to_all(queries, "inner", split_axis=1, concat_axis=0, tiled=True),
        lax.all_to_all(key_rows, "inner", split_axis=1, concat_axis=0, tiled=True),
        lax.all_to_all(value_rows, "inner", split_axis=1, concat_axis=0, tiled=True),
        lax.all_to_all(out_grad, "inner", split_axis=1, concat_axis=0, tiled=True),
        lax.all_to_all(beta_logit, "inner", split_axis=1, concat_axis=0, tiled=True),
        lax.all_to_all(log_gate, "inner", split_axis=1, concat_axis=0, tiled=True),
    )
    pieces = prepare(arrived[0], arrived[1], arrived[2], arrived[3], arrived[4], arrived[5])
    start_state = block_states[0]
    turned, grad_start, finish = block_pullback(pieces, start_state)
    gathered = (
        lax.all_gather(turned[None], "outer", axis=0, tiled=True),
        lax.all_gather(grad_start[None], "outer", axis=0, tiled=True),
    )
    incoming = fold_later(gathered[0], gathered[1], lax.axis_index("outer"))
    gradients = finish(incoming)
    result = (
        lax.all_to_all(merge_heads(gradients[0]), "inner", split_axis=0, concat_axis=1, tiled=True),
        lax.all_to_all(merge_heads(gradients[1]), "inner", split_axis=0, concat_axis=1, tiled=True),
        lax.all_to_all(merge_heads(gradients[2]), "inner", split_axis=0, concat_axis=1, tiled=True),
        lax.all_to_all(
            gradients[3].T.astype(jnp.bfloat16), "inner", split_axis=0, concat_axis=1, tiled=True
        ),
        lax.all_to_all(
            gradients[4].T.astype(jnp.bfloat16), "inner", split_axis=0, concat_axis=1, tiled=True
        ),
    )
    return (result[0], result[1], result[2], result[3], result[4])


def solution(mesh):
    return jax.shard_map(
        shards,
        mesh=mesh,
        in_specs=(
            P(("outer", "inner"), None),
            P(("outer", "inner"), None),
            P(("outer", "inner"), None),
            P(("outer", "inner"), None),
            P(("outer", "inner"), None),
            P(("outer", "inner"), None),
            P("outer", "inner", None, None),
        ),
        out_specs=(
            P(("outer", "inner"), None),
            P(("outer", "inner"), None),
            P(("outer", "inner"), None),
            P(("outer", "inner"), None),
            P(("outer", "inner"), None),
        ),
        check_vma=False,
    )
```

profile of v0, /device:TPU:0, one launch (start us, length us, event | category | flops | bytes accessed | tf_op | source)
XLA Modules:
  0.0 874.6 jit_solution(8195031747380546615)
XLA Ops:
  0.6 11.9 %all_to_all.164 = bf16[128,8,2]{0,2,1:T(2,128)(2,1)S(1)} all-to-all(bf16[128,8,2]{0,2,1:T(2,128)(2,1)} %bitcast.638), channel_id=1, replica_groups=mesh['outer'=4,'inner'=8] {'inner'}, dimensions={1} | all-to-all | bytes 8192 | tf_op jit(solution)/shard_map/all_to_all | solution.py:152
  12.6 3.3 all-to-all-start
  18.0 3.3 all-to-all-done
  21.3 3.6 all-to-all-start.1
  26.0 14.3 %all-to-all-done.1 = bf16[128,8,256]{0,2,1:T(8,128)(2,1)S(1)} async-done(((bf16[128,8,256]{0,2,1:T(8,128)(2,1)}), bf16[128,8,256]{0,2,1:T(8,128)(2,1)S(1)}, u32[]{:S(2)}, u32[]{:S(2)}) %all-to-all-start.1) | async-done | bytes 524320 | tf_op jit(solution)/shard_map/all_to_all | solution.py:149
  40.2 3.5 all-to-all-start.4
  47.6 11.4 %all-to-all-done.4 = bf16[128,8,256]{0,2,1:T(8,128)(2,1)S(1)} async-done(((bf16[128,8,256]{0,2,1:T(8,128)(2,1)}), bf16[128,8,256]{0,2,1:T(8,128)(2,1)S(1)}, u32[]{:S(2)}, u32[]{:S(2)}) %all-to-all-start.4) | async-done | bytes 524320 | tf_op jit(solution)/shard_map/all_to_all | solution.py:148
  59.0 4.1 all-to-all-start.3
  64.4 14.2 %all-to-all-done.3 = bf16[128,8,256]{0,2,1:T(8,128)(2,1)} async-done(((bf16[128,8,256]{0,2,1:T(8,128)(2,1)}), bf16[128,8,256]{0,2,1:T(8,128)(2,1)}, u32[]{:S(2)}, u32[]{:S(2)}) %all-to-all-start.3) | async-done | bytes 524320 | tf_op jit(solution)/shard_map/all_to_all | solution.py:150
  78.5 4.3 all-to-all-start.5
  91.0 2.5 copy.350
  96.3 2.4 reshape.533
  98.6 2.6 copy.347
  106.2 2.4 reshape.534
  108.6 2.6 copy.353
  111.2 2.3 copy.359
  113.6 269.3 %while.108 = (s32[]{:T(128)}, f32[2,128,128]{2,1,0:T(8,128)S(1)}, f32[2,128,128]{2,1,0:T(8,128)S(1)}, f32[2,128,128]{1,2,0:T(8,128)S(1)}, f32[8,2,128,128]{3,2,1...) while((s32[]{:T(128)}, f32[2,128,128]{2,1,0:T(8,128)S(1)}, ...), condition=%wide.region_4.5_spmd.clone.clone, body=%wide.region_2.4_spmd.clone.clone.sunk | while | flops 555172992 | bytes 8843675 | solution.py:85
  118.0 19.7 %custom-call.48 = f32[2,1,128,128]{2,3,1,0:T(8,128)S(1)} custom-call(f32[2,1,128,128]{3,2,1,0:T(8,128)S(1)} %get-tuple-element.3072), custom_call_target="InvertDiagBlocksLowerTriangular" | custom-call | tf_op jit(solution)/shard_map/jvp()/while/body/eval_jaxpr/triangular_solve | solution.py:35
  151.6 19.7 %custom-call.48 = f32[2,1,128,128]{2,3,1,0:T(8,128)S(1)} custom-call(f32[2,1,128,128]{3,2,1,0:T(8,128)S(1)} %get-tuple-element.3072), custom_call_target="InvertDiagBlocksLowerTriangular" | custom-call | tf_op jit(solution)/shard_map/jvp()/while/body/eval_jaxpr/triangular_solve | solution.py:35
  185.3 19.7 %custom-call.48 = f32[2,1,128,128]{2,3,1,0:T(8,128)S(1)} custom-call(f32[2,1,128,128]{3,2,1,0:T(8,128)S(1)} %get-tuple-element.3072), custom_call_target="InvertDiagBlocksLowerTriangular" | custom-call | tf_op jit(solution)/shard_map/jvp()/while/body/eval_jaxpr/triangular_solve | solution.py:35
  219.0 19.7 %custom-call.48 = f32[2,1,128,128]{2,3,1,0:T(8,128)S(1)} custom-call(f32[2,1,128,128]{3,2,1,0:T(8,128)S(1)} %get-tuple-element.3072), custom_call_target="InvertDiagBlocksLowerTriangular" | custom-call | tf_op jit(solution)/shard_map/jvp()/while/body/eval_jaxpr/triangular_solve | solution.py:35
  252.6 19.7 %custom-call.48 = f32[2,1,128,128]{2,3,1,0:T(8,128)S(1)} custom-call(f32[2,1,128,128]{3,2,1,0:T(8,128)S(1)} %get-tuple-element.3072), custom_call_target="InvertDiagBlocksLowerTriangular" | custom-call | tf_op jit(solution)/shard_map/jvp()/while/body/eval_jaxpr/triangular_solve | solution.py:35
  286.3 19.7 %custom-call.48 = f32[2,1,128,128]{2,3,1,0:T(8,128)S(1)} custom-call(f32[2,1,128,128]{3,2,1,0:T(8,128)S(1)} %get-tuple-element.3072), custom_call_target="InvertDiagBlocksLowerTriangular" | custom-call | tf_op jit(solution)/shard_map/jvp()/while/body/eval_jaxpr/triangular_solve | solution.py:35
  319.9 19.7 %custom-call.48 = f32[2,1,128,128]{2,3,1,0:T(8,128)S(1)} custom-call(f32[2,1,128,128]{3,2,1,0:T(8,128)S(1)} %get-tuple-element.3072), custom_call_target="InvertDiagBlocksLowerTriangular" | custom-call | tf_op jit(solution)/shard_map/jvp()/while/body/eval_jaxpr/triangular_solve | solution.py:35
  353.6 19.7 %custom-call.48 = f32[2,1,128,128]{2,3,1,0:T(8,128)S(1)} custom-call(f32[2,1,128,128]{3,2,1,0:T(8,128)S(1)} %get-tuple-element.3072), custom_call_target="InvertDiagBlocksLowerTriangular" | custom-call | tf_op jit(solution)/shard_map/jvp()/while/body/eval_jaxpr/triangular_solve | solution.py:35
  383.0 11.4 %all-gather = f32[8,128,128]{2,1,0:T(8,128)} all-gather(f32[2,128,128]{2,1,0:T(8,128)S(1)} %bitcast.630), channel_id=2, replica_groups=mesh['outer'=4,'inner'=8] {'outer'}, dimensions={0}, use_global_device_ids=true | all-gather | bytes 655360 | tf_op jit(solution)/shard_map/all_gather | solution.py:159
  394.5 10.2 %all-gather.1 = f32[8,128,128]{2,1,0:T(8,128)} all-gather(f32[2,128,128]{2,1,0:T(8,128)S(1)} %copy.361), channel_id=3, replica_groups=mesh['outer'=4,'inner'=8] {'outer'}, dimensions={0}, use_global_device_ids=true | all-gather | bytes 655360 | tf_op jit(solution)/shard_map/all_gather | solution.py:160
  404.7 5.2 while.107
  412.0 380.4 %while.106 = (s32[]{:T(128)}, f32[2,128,128]{2,1,0:T(8,128)S(1)}, f32[8,2,128,128]{3,2,0,1:T(8,128)}, f32[8,2,128,128]{3,2,0,1:T(8,128)}, bf16[8,2,128,128]{3,2,...) while((s32[]{:T(128)}, f32[2,128,128]{2,1,0:T(8,128)S(1)}, ...), condition=%wide.region_18.19_spmd.clone.clone, body=%wide.region_7.18_spmd.clone.clone.sunk | while | flops 857327744 | bytes 11667445 | solution.py:85
  416.9 19.7 %custom-call.47 = f32[2,1,128,128]{2,3,1,0:T(8,128)S(1)} custom-call(f32[2,1,128,128]{3,2,1,0:T(8,128)S(1)} %add_bitcast_fusion.4), custom_call_target="InvertDiagBlocksLowerTriangular" | custom-call | tf_op jit(solution)/shard_map/transpose(jvp())/while/body/eval_jaxpr/triangular_solve | solution.py:35
  464.4 19.7 %custom-call.47 = f32[2,1,128,128]{2,3,1,0:T(8,128)S(1)} custom-call(f32[2,1,128,128]{3,2,1,0:T(8,128)S(1)} %add_bitcast_fusion.4), custom_call_target="InvertDiagBlocksLowerTriangular" | custom-call | tf_op jit(solution)/shard_map/transpose(jvp())/while/body/eval_jaxpr/triangular_solve | solution.py:35
  512.0 19.7 %custom-call.47 = f32[2,1,128,128]{2,3,1,0:T(8,128)S(1)} custom-call(f32[2,1,128,128]{3,2,1,0:T(8,128)S(1)} %add_bitcast_fusion.4), custom_call_target="InvertDiagBlocksLowerTriangular" | custom-call | tf_op jit(solution)/shard_map/transpose(jvp())/while/body/eval_jaxpr/triangular_solve | solution.py:35
  559.6 19.7 %custom-call.47 = f32[2,1,128,128]{2,3,1,0:T(8,128)S(1)} custom-call(f32[2,1,128,128]{3,2,1,0:T(8,128)S(1)} %add_bitcast_fusion.4), custom_call_target="InvertDiagBlocksLowerTriangular" | custom-call | tf_op jit(solution)/shard_map/transpose(jvp())/while/body/eval_jaxpr/triangular_solve | solution.py:35
  607.1 19.7 %custom-call.47 = f32[2,1,128,128]{2,3,1,0:T(8,128)S(1)} custom-call(f32[2,1,128,128]{3,2,1,0:T(8,128)S(1)} %add_bitcast_fusion.4), custom_call_target="InvertDiagBlocksLowerTriangular" | custom-call | tf_op jit(solution)/shard_map/transpose(jvp())/while/body/eval_jaxpr/triangular_solve | solution.py:35
  654.7 19.7 %custom-call.47 = f32[2,1,128,128]{2,3,1,0:T(8,128)S(1)} custom-call(f32[2,1,128,128]{3,2,1,0:T(8,128)S(1)} %add_bitcast_fusion.4), custom_call_target="InvertDiagBlocksLowerTriangular" | custom-call | tf_op jit(solution)/shard_map/transpose(jvp())/while/body/eval_jaxpr/triangular_solve | solution.py:35
  702.2 19.7 %custom-call.47 = f32[2,1,128,128]{2,3,1,0:T(8,128)S(1)} custom-call(f32[2,1,128,128]{3,2,1,0:T(8,128)S(1)} %add_bitcast_fusion.4), custom_call_target="InvertDiagBlocksLowerTriangular" | custom-call | tf_op jit(solution)/shard_map/transpose(jvp())/while/body/eval_jaxpr/triangular_solve | solution.py:35
  749.8 19.7 %custom-call.47 = f32[2,1,128,128]{2,3,1,0:T(8,128)S(1)} custom-call(f32[2,1,128,128]{3,2,1,0:T(8,128)S(1)} %add_bitcast_fusion.4), custom_call_target="InvertDiagBlocksLowerTriangular" | custom-call | tf_op jit(solution)/shard_map/transpose(jvp())/while/body/eval_jaxpr/triangular_solve | solution.py:35
  792.4 2.6 copy.376
  797.0 4.8 all-to-all-start.9
  801.8 5.5 all-to-all-done.9
  807.3 3.3 all-to-all-start.10
  813.0 3.0 all-to-all-done.10
  816.0 3.5 all-to-all-start.7
  822.5 12.3 %all-to-all-done.7 = bf16[8,128,256]{1,2,0:T(8,128)(2,1)S(1)} async-done(((bf16[8,128,256]{1,2,0:T(8,128)(2,1)}), bf16[8,128,256]{1,2,0:T(8,128)(2,1)S(1)}, u32[]{:S(2)}, u32[]{:S(2)}) %all-to-all-start.7) | async-done | bytes 524320 | tf_op jit(solution)/shard_map/all_to_all | solution.py:166
  834.8 3.5 all-to-all-start.6
  839.5 14.1 %all-to-all-done.6 = bf16[8,128,256]{1,2,0:T(8,128)(2,1)S(1)} async-done(((bf16[8,128,256]{1,2,0:T(8,128)(2,1)}), bf16[8,128,256]{1,2,0:T(8,128)(2,1)S(1)}, u32[]{:S(2)}, u32[]{:S(2)}) %all-to-all-start.6) | async-done | bytes 524320 | tf_op jit(solution)/shard_map/all_to_all | solution.py:165
  853.6 3.5 all-to-all-start.8
  859.1 13.3 %all-to-all-done.8 = bf16[8,128,256]{1,2,0:T(8,128)(2,1)S(1)} async-done(((bf16[8,128,256]{1,2,0:T(8,128)(2,1)}), bf16[8,128,256]{1,2,0:T(8,128)(2,1)S(1)}, u32[]{:S(2)}, u32[]{:S(2)}) %all-to-all-start.8) | async-done | bytes 524320 | tf_op jit(solution)/shard_map/all_to_all | solution.py:167
  (613 shorter events, 376.5 us)
Async XLA Ops:
  0.6 24.3 %copy-start.5 = (bf16[128,2048]{1,0:T(8,128)(2,1)S(1)}, bf16[128,2048]{1,0:T(8,128)(2,1)}, u32[]{:S(2)}) copy-start(bf16[128,2048]{1,0:T(8,128)(2,1)} %param.13) | copy-start | bytes 1572868
  12.6 8.7 all-to-all-start
  15.9 28.0 %copy-start.6 = (bf16[128,2048]{1,0:T(8,128)(2,1)S(1)}, bf16[128,2048]{1,0:T(8,128)(2,1)}, u32[]{:S(2)}) copy-start(bf16[128,2048]{1,0:T(8,128)(2,1)} %param.15) | copy-start | bytes 1572868
  21.3 23.6 %copy-start.7 = (bf16[128,2048]{1,0:T(8,128)(2,1)S(1)}, bf16[128,2048]{1,0:T(8,128)(2,1)}, u32[]{:S(2)}) copy-start(bf16[128,2048]{1,0:T(8,128)(2,1)} %param.18) | copy-start | bytes 1572868
  21.3 18.9 %all-to-all-start.1 = ((bf16[128,8,256]{0,2,1:T(8,128)(2,1)}), bf16[128,8,256]{0,2,1:T(8,128)(2,1)S(1)}, u32[]{:S(2)}, u32[]{:S(2)}) async-start(bf16[128,8,256]{0,2,1:T(8,128)(2,1)} %bitcast.6), calls=%async_computation.1 | async-start | bytes 1048576 | tf_op jit(solution)/shard_map/all_to_all | solution.py:149
  40.2 18.8 %all-to-all-start.4 = ((bf16[128,8,256]{0,2,1:T(8,128)(2,1)}), bf16[128,8,256]{0,2,1:T(8,128)(2,1)S(1)}, u32[]{:S(2)}, u32[]{:S(2)}) async-start(bf16[128,8,256]{0,2,1:T(8,128)(2,1)} %bitcast.20), calls=%async_computation.4 | async-start | bytes 1048576 | tf_op jit(solution)/shard_map/all_to_all | solution.py:148
  59.0 19.5 %all-to-all-start.3 = ((bf16[128,8,256]{0,2,1:T(8,128)(2,1)}), bf16[128,8,256]{0,2,1:T(8,128)(2,1)}, u32[]{:S(2)}, u32[]{:S(2)}) async-start(bf16[128,8,256]{0,2,1:T(8,128)(2,1)} %bitcast.15), calls=%async_computation.3 | async-start | bytes 1048576 | tf_op jit(solution)/shard_map/all_to_all | solution.py:150
  64.1 14.4 %copy-start.1 = (f32[1024,2,128]{0,2,1:T(8,128)}, f32[1024,2,128]{0,2,1:T(8,128)S(1)}, u32[]{:S(2)}) copy-start(f32[1024,2,128]{0,2,1:T(8,128)S(1)} %reshape.528) | copy-start | bytes 3145732
  78.5 25.0 %all-to-all-start.5 = ((bf16[128,8,256]{0,2,1:T(8,128)(2,1)}), bf16[128,8,256]{0,2,1:T(8,128)(2,1)}, u32[]{:S(2)}, u32[]{:S(2)}) async-start(bf16[128,8,256]{0,2,1:T(8,128)(2,1)} %bitcast.622), calls=%async_computation.5 | async-start | bytes 1048576 | tf_op jit(solution)/shard_map/all_to_all | solution.py:151
  85.2 1.5 copy-start.3
  108.6 5.0 copy-start
  792.4 2.7 copy-start.2
  797.0 10.3 %all-to-all-start.9 = ((bf16[8,128,2]{1,2,0:T(2,128)(2,1)}), bf16[8,128,2]{1,2,0:T(2,128)(2,1)S(1)}, u32[]{:S(2)}, u32[]{:S(2)}) async-start(bf16[8,128,2]{1,2,0:T(2,128)(2,1)} %fusion.167), calls=%async_computation.9 | async-start | bytes 8192 | tf_op jit(solution)/shard_map/all_to_all | solution.py:168
  807.3 8.7 all-to-all-start.10
  816.0 18.8 %all-to-all-start.7 = ((bf16[8,128,256]{1,2,0:T(8,128)(2,1)}), bf16[8,128,256]{1,2,0:T(8,128)(2,1)S(1)}, u32[]{:S(2)}, u32[]{:S(2)}) async-start(bf16[8,128,256]{1,2,0:T(8,128)(2,1)} %copy.378), calls=%async_computation.7 | async-start | bytes 1048576 | tf_op jit(solution)/shard_map/all_to_all | solution.py:166
  821.5 16.8 %copy-start.4 = (bf16[8,2,128,128]{3,2,0,1:T(8,128)(2,1)S(1)}, bf16[8,2,128,128]{3,2,0,1:T(8,128)(2,1)}, u32[]{:S(2)}) copy-start(bf16[8,2,128,128]{3,2,0,1:T(8,128)(2,1)} %get-tuple-element.1507) | copy-start | bytes 1572868
  834.8 18.8 %all-to-all-start.6 = ((bf16[8,128,256]{1,2,0:T(8,128)(2,1)}), bf16[8,128,256]{1,2,0:T(8,128)(2,1)S(1)}, u32[]{:S(2)}, u32[]{:S(2)}) async-start(bf16[8,128,256]{1,2,0:T(8,128)(2,1)} %copy.374), calls=%async_computation.6 | async-start | bytes 1048576 | tf_op jit(solution)/shard_map/all_to_all | solution.py:165
  853.6 18.8 %all-to-all-start.8 = ((bf16[8,128,256]{1,2,0:T(8,128)(2,1)}), bf16[8,128,256]{1,2,0:T(8,128)(2,1)S(1)}, u32[]{:S(2)}, u32[]{:S(2)}) async-start(bf16[8,128,256]{1,2,0:T(8,128)(2,1)} %copy.381), calls=%async_computation.8 | async-start | bytes 1048576 | tf_op jit(solution)/shard_map/all_to_all | solution.py:167
where the time goes:
time: 880 us; the launch traced here: 875 us
  other arithmetic  406 us (46%)
  matrix products  225 us (26%)
  waiting for transfers between devices  91.2 us (10%)
  local copies, waits for them, and re-layouts  77.8 us (9%)
  starting transfers between devices  37.5 us (4%)
  blocking collectives  33.5 us (4%)
    another operation x80, other arithmetic, group_step(): lax.linalg.triangular_solve(unit_lower, right_side, left_side=True, lower...  332 us
    dot_general x24, matrix products, group_step(): jnp.einsum('hid,hjd->hij', query_part, key_part, precision=precise)  38.8 us
    dynamic_update_slice x48, other arithmetic, block_forward(): lax.scan(group_step, (start_state, identity, grad_zero), inputs)  38.2 us
    dot_general x24, matrix products, group_step(): key_gram = jnp.einsum('hid,hjd->hij', key_part, key_part, precision=precise)  28.3 us
    dot_general x24, matrix products, group_step(): jnp.einsum('hcd,hde->hce', write_keys, state_now, precision=precise)  28.1 us
    dot_general x24, matrix products, group_step(): jnp.einsum('hcd,hce->hde', tail_keys, new_values, precision=precise)  25.2 us
    dot_general x16, matrix products, group_step(): jnp.einsum('hij,hje->hie', scores, new_values, precision=precise)  23.9 us
    dot_general x16, matrix products, group_step(): jnp.einsum('hcd,hde->hce', grown_queries, state_now, precision=precise)  21.9 us
  transfers between devices with their start and end apart: 10, of which 9 were waited for; matrix products, arithmetic and copies ran while one was open for 4% of the time, Pallas kernels for 0%

commit v1 on v0

--- a/solution.py
+++ b/solution.py
@@ -7,6 +7,22 @@
 DV = 128
 GROUP = 128
 precise = lax.Precision.HIGHEST
+
+
+def swapped_with_each(x, axis, split, join):
+    ways, here = (lax.axis_size(axis), lax.axis_index(axis))
+    width = x.shape[split] // ways
+    dims = list(x.shape)
+    dims[split] = width
+    height = dims[join]
+    dims[join] = height * ways
+    full = jnp.zeros(dims, x.dtype)
+    for mask in range(ways):
+        part = lax.dynamic_slice_in_dim(x, (here ^ mask) * width, width, axis=split)
+        if mask:
+            part = lax.ppermute(part, axis, [(d, d ^ mask) for d in range(ways)])
+        full = lax.dynamic_update_slice_in_dim(full, part, (here ^ mask) * height, axis=join)
+    return full
 
 
 def unit_rows(matrix):
@@ -146,7 +162,7 @@
 def shards(queries, key_rows, value_rows, beta_logit, log_gate, out_grad, block_states):
     arrived = (
         lax.all_to_all(queries, "inner", split_axis=1, concat_axis=0, tiled=True),
-        lax.all_to_all(key_rows, "inner", split_axis=1, concat_axis=0, tiled=True),
+        swapped_with_each(key_rows, "inner", 1, 0),
         lax.all_to_all(value_rows, "inner", split_axis=1, concat_axis=0, tiled=True),
         lax.all_to_all(out_grad, "inner", split_axis=1, concat_axis=0, tiled=True),
         lax.all_to_all(beta_logit, "inner", split_axis=1, concat_axis=0, tiled=True),

time: 880 us -> 1070 us (1.22)
  other arithmetic: 406 us -> 488 us
  local copies, waits for them, and re-layouts: 77.8 us -> 141 us
  matrix products: 225 us -> 274 us
  blocking collectives: 33.5 us -> 21.6 us
  starting transfers between devices: 37.5 us -> 48.8 us
  waiting for transfers between devices: 91.2 us -> 80.2 us
    another operation x24, other arithmetic: 13.3 us -> 33.1 us  [group_step(): cumulative = jnp.cumsum(gate_part, axis=1)]
    dynamic_update_slice x48, other arithmetic: 38.2 us -> 57.9 us  [block_forward(): lax.scan(group_step, (start_state, identity, grad_zero), inputs)]
    another operation x80, other arithmetic: 332 us -> 349 us  [group_step(): lax.linalg.triangular_solve(unit_lower, right_side, left_side=True, lower...]
    while x12 -> x188, local copies, waits for them, and re-layouts: 0.13 us -> 16.7 us
    another operation x24, matrix products: 15.2 us -> 28.1 us  [group_step(): lax.linalg.triangular_solve(unit_lower, right_side, left_side=True, lower...]
    all_to_all x1 -> x0, blocking collectives: 11.9 us -> none  [shards(): lax.all_to_all(beta_logit, 'inner', split_axis=1, concat_axis=0, tiled=True)]
    dot_general x8, matrix products: 2.19 us -> 13.7 us  [group_step(): jnp.einsum('hji,hje->hie', transition, projected, precision=precise)]
    all_to_all x1, waiting for transfers between devices: 14.3 us -> 3.03 us  [shards(): lax.all_to_all(beta_logit, 'inner', split_axis=1, concat_axis=0, tiled=True)]
  transfers between devices with their start and end apart: 10 -> 17, of which waited for: 9 -> 9; matrix products, arithmetic and copies ran while one was open for 4% -> 3% of each run, Pallas kernels for 0% -> 0%
where the time goes in v1:
time: 1070 us; the launch traced here: 1060 us
  other arithmetic  488 us (46%)
  matrix products  274 us (26%)
  local copies, waits for them, and re-layouts  141 us (13%)
  waiting for transfers between devices  80.2 us (7%)
  starting transfers between devices  48.8 us (5%)
  blocking collectives  21.6 us (2%)
    another operation x80, other arithmetic, group_step(): lax.linalg.triangular_solve(unit_lower, right_side, left_side=True, lower...  349 us
    dynamic_update_slice x48, other arithmetic, block_forward(): lax.scan(group_step, (start_state, identity, grad_zero), inputs)  57.9 us
    dot_general x24, matrix products, group_step(): jnp.einsum('hid,hjd->hij', query_part, key_part, precision=precise)  39.3 us
    dot_general x24, matrix products, group_step(): jnp.einsum('hcd,hce->hde', tail_keys, new_values, precision=precise)  34 us
    another operation x24, other arithmetic, group_step(): cumulative = jnp.cumsum(gate_part, axis=1)  33.1 us
    dot_general x16, matrix products, group_step(): jnp.einsum('hij,hje->hie', scores, new_values, precision=precise)  28.7 us
    dot_general x24, matrix products, group_step(): key_gram = jnp.einsum('hid,hjd->hij', key_part, key_part, precision=precise)  28.2 us
    dot_general x24, matrix products, group_step(): jnp.einsum('hcd,hde->hce', write_keys, state_now, precision=precise)  28.2 us
  transfers between devices with their start and end apart: 17, of which 9 were waited for; matrix products, arithmetic and copies ran while one was open for 3% of the time, Pallas kernels for 0%

profile of v1, /device:TPU:0, one launch (start us, length us, event | category | flops | bytes accessed | tf_op | source)
XLA Modules:
  0.0 1057.4 jit_solution(9382843355796998001)
XLA Ops:
  2.6 2.7 collective-permute-start.1
  5.7 2.8 collective-permute-start.3
  8.7 4.9 all-to-all-start.1
  16.1 3.0 all-to-all-done.1
  19.1 3.3 all-to-all-start
  24.0 3.8 all-to-all-done
  27.8 3.5 all-to-all-start.3
  35.6 3.8 collective-permute-start.5
  39.6 10.3 all-to-all-done.3
  49.9 4.2 all-to-all-start.2
  55.6 13.8 %all-to-all-done.2 = bf16[128,8,256]{0,2,1:T(8,128)(2,1)} async-done(((bf16[128,8,256]{0,2,1:T(8,128)(2,1)}), bf16[128,8,256]{0,2,1:T(8,128)(2,1)}, u32[]{:S(2)}, u32[]{:S(2)}) %all-to-all-start.2) | async-done | bytes 524320 | tf_op jit(solution)/shard_map/all_to_all | solution.py:166
  69.4 4.3 all-to-all-start.4
  95.7 2.6 copy.381
  102.5 346.6 %while.108 = (s32[]{:T(128)}, f32[2,128,128]{2,1,0:T(8,128)S(1)}, f32[2,128,128]{2,1,0:T(8,128)}, f32[2,128,128]{1,2,0:T(8,128)}, f32[8,2,128,128]{3,2,1,0:T(8,1...) while((s32[]{:T(128)}, f32[2,128,128]{2,1,0:T(8,128)S(1)}, ...), condition=%wide.region_4.5_spmd.clone.clone, body=%wide.region_2.4_spmd.clone.clone.sunk | while | flops 555172992 | bytes 8860807 | solution.py:101
  109.4 21.1 %custom-call.48 = f32[2,1,128,128]{2,3,1,0:T(8,128)} custom-call(f32[2,1,128,128]{3,2,1,0:T(8,128)} %get-tuple-element.3080), custom_call_target="InvertDiagBlocksLowerTriangular" | custom-call | tf_op jit(solution)/shard_map/jvp()/while/body/eval_jaxpr/triangular_solve | solution.py:51
  151.9 21.1 %custom-call.48 = f32[2,1,128,128]{2,3,1,0:T(8,128)} custom-call(f32[2,1,128,128]{3,2,1,0:T(8,128)} %get-tuple-element.3080), custom_call_target="InvertDiagBlocksLowerTriangular" | custom-call | tf_op jit(solution)/shard_map/jvp()/while/body/eval_jaxpr/triangular_solve | solution.py:51
  195.4 21.1 %custom-call.48 = f32[2,1,128,128]{2,3,1,0:T(8,128)} custom-call(f32[2,1,128,128]{3,2,1,0:T(8,128)} %get-tuple-element.3080), custom_call_target="InvertDiagBlocksLowerTriangular" | custom-call | tf_op jit(solution)/shard_map/jvp()/while/body/eval_jaxpr/triangular_solve | solution.py:51
  238.8 21.1 %custom-call.48 = f32[2,1,128,128]{2,3,1,0:T(8,128)} custom-call(f32[2,1,128,128]{3,2,1,0:T(8,128)} %get-tuple-element.3080), custom_call_target="InvertDiagBlocksLowerTriangular" | custom-call | tf_op jit(solution)/shard_map/jvp()/while/body/eval_jaxpr/triangular_solve | solution.py:51
  282.3 21.1 %custom-call.48 = f32[2,1,128,128]{2,3,1,0:T(8,128)} custom-call(f32[2,1,128,128]{3,2,1,0:T(8,128)} %get-tuple-element.3080), custom_call_target="InvertDiagBlocksLowerTriangular" | custom-call | tf_op jit(solution)/shard_map/jvp()/while/body/eval_jaxpr/triangular_solve | solution.py:51
  325.7 21.1 %custom-call.48 = f32[2,1,128,128]{2,3,1,0:T(8,128)} custom-call(f32[2,1,128,128]{3,2,1,0:T(8,128)} %get-tuple-element.3080), custom_call_target="InvertDiagBlocksLowerTriangular" | custom-call | tf_op jit(solution)/shard_map/jvp()/while/body/eval_jaxpr/triangular_solve | solution.py:51
  369.2 21.1 %custom-call.48 = f32[2,1,128,128]{2,3,1,0:T(8,128)} custom-call(f32[2,1,128,128]{3,2,1,0:T(8,128)} %get-tuple-element.3080), custom_call_target="InvertDiagBlocksLowerTriangular" | custom-call | tf_op jit(solution)/shard_map/jvp()/while/body/eval_jaxpr/triangular_solve | solution.py:51
  412.6 21.1 %custom-call.48 = f32[2,1,128,128]{2,3,1,0:T(8,128)} custom-call(f32[2,1,128,128]{3,2,1,0:T(8,128)} %get-tuple-element.3080), custom_call_target="InvertDiagBlocksLowerTriangular" | custom-call | tf_op jit(solution)/shard_map/jvp()/while/body/eval_jaxpr/triangular_solve | solution.py:51
  450.1 11.4 %all-gather = f32[8,128,128]{2,1,0:T(8,128)} all-gather(f32[2,128,128]{2,1,0:T(8,128)S(1)} %bitcast.636), channel_id=2, replica_groups=mesh['outer'=4,'inner'=8] {'outer'}, dimensions={0}, use_global_device_ids=true | all-gather | bytes 655360 | tf_op jit(solution)/shard_map/all_gather | solution.py:175
  462.4 10.2 all-gather.1
  472.6 5.2 while.107
  480.6 496.8 %while.106 = (s32[]{:T(128)}, f32[2,128,128]{2,1,0:T(8,128)S(1)}, f32[8,2,128,128]{3,2,0,1:T(8,128)}, f32[8,2,128,128]{3,2,0,1:T(8,128)}, bf16[8,2,128,128]{3,2,...) while((s32[]{:T(128)}, f32[2,128,128]{2,1,0:T(8,128)S(1)}, ...), condition=%wide.region_18.19_spmd.clone.clone, body=%wide.region_7.18_spmd.clone.clone.sunk | while | flops 857327744 | bytes 11688065 | solution.py:101
  485.5 19.7 %custom-call.47 = f32[2,1,128,128]{2,3,1,0:T(8,128)S(1)} custom-call(f32[2,1,128,128]{3,2,1,0:T(8,128)S(1)} %add_bitcast_fusion.4), custom_call_target="InvertDiagBlocksLowerTriangular" | custom-call | tf_op jit(solution)/shard_map/transpose(jvp())/while/body/eval_jaxpr/triangular_solve | solution.py:51
  516.6 2.6 fusion.276
  547.6 19.7 %custom-call.47 = f32[2,1,128,128]{2,3,1,0:T(8,128)S(1)} custom-call(f32[2,1,128,128]{3,2,1,0:T(8,128)S(1)} %add_bitcast_fusion.4), custom_call_target="InvertDiagBlocksLowerTriangular" | custom-call | tf_op jit(solution)/shard_map/transpose(jvp())/while/body/eval_jaxpr/triangular_solve | solution.py:51
  578.6 2.6 fusion.276
  609.6 19.7 %custom-call.47 = f32[2,1,128,128]{2,3,1,0:T(8,128)S(1)} custom-call(f32[2,1,128,128]{3,2,1,0:T(8,128)S(1)} %add_bitcast_fusion.4), custom_call_target="InvertDiagBlocksLowerTriangular" | custom-call | tf_op jit(solution)/shard_map/transpose(jvp())/while/body/eval_jaxpr/triangular_solve | solution.py:51
  671.8 19.7 %custom-call.47 = f32[2,1,128,128]{2,3,1,0:T(8,128)S(1)} custom-call(f32[2,1,128,128]{3,2,1,0:T(8,128)S(1)} %add_bitcast_fusion.4), custom_call_target="InvertDiagBlocksLowerTriangular" | custom-call | tf_op jit(solution)/shard_map/transpose(jvp())/while/body/eval_jaxpr/triangular_solve | solution.py:51
  734.0 19.7 %custom-call.47 = f32[2,1,128,128]{2,3,1,0:T(8,128)S(1)} custom-call(f32[2,1,128,128]{3,2,1,0:T(8,128)S(1)} %add_bitcast_fusion.4), custom_call_target="InvertDiagBlocksLowerTriangular" | custom-call | tf_op jit(solution)/shard_map/transpose(jvp())/while/body/eval_jaxpr/triangular_solve | solution.py:51
  765.0 2.6 fusion.276
  796.0 19.7 %custom-call.47 = f32[2,1,128,128]{2,3,1,0:T(8,128)S(1)} custom-call(f32[2,1,128,128]{3,2,1,0:T(8,128)S(1)} %add_bitcast_fusion.4), custom_call_target="InvertDiagBlocksLowerTriangular" | custom-call | tf_op jit(solution)/shard_map/transpose(jvp())/while/body/eval_jaxpr/triangular_solve | solution.py:51
  827.1 2.6 fusion.276
  858.1 19.7 %custom-call.47 = f32[2,1,128,128]{2,3,1,0:T(8,128)S(1)} custom-call(f32[2,1,128,128]{3,2,1,0:T(8,128)S(1)} %add_bitcast_fusion.4), custom_call_target="InvertDiagBlocksLowerTriangular" | custom-call | tf_op jit(solution)/shard_map/transpose(jvp())/while/body/eval_jaxpr/triangular_solve | solution.py:51
  920.3 19.7 %custom-call.47 = f32[2,1,128,128]{2,3,1,0:T(8,128)S(1)} custom-call(f32[2,1,128,128]{3,2,1,0:T(8,128)S(1)} %add_bitcast_fusion.4), custom_call_target="InvertDiagBlocksLowerTriangular" | custom-call | tf_op jit(solution)/shard_map/transpose(jvp())/while/body/eval_jaxpr/triangular_solve | solution.py:51
  979.8 4.8 all-to-all-start.8
  984.6 5.5 all-to-all-done.8
  990.1 3.3 all-to-all-start.9
  994.6 4.3 all-to-all-done.9
  998.8 3.5 all-to-all-start.6
  1005.4 12.2 %all-to-all-done.6 = bf16[8,128,256]{1,2,0:T(8,128)(2,1)S(1)} async-done(((bf16[8,128,256]{1,2,0:T(8,128)(2,1)}), bf16[8,128,256]{1,2,0:T(8,128)(2,1)S(1)}, u32[]{:S(2)}, u32[]{:S(2)}) %all-to-all-start.6) | async-done | bytes 524320 | tf_op jit(solution)/shard_map/all_to_all | solution.py:182
  1017.6 3.5 all-to-all-start.5
  1022.4 14.0 %all-to-all-done.5 = bf16[8,128,256]{1,2,0:T(8,128)(2,1)S(1)} async-done(((bf16[8,128,256]{1,2,0:T(8,128)(2,1)}), bf16[8,128,256]{1,2,0:T(8,128)(2,1)S(1)}, u32[]{:S(2)}, u32[]{:S(2)}) %all-to-all-start.5) | async-done | bytes 524320 | tf_op jit(solution)/shard_map/all_to_all | solution.py:181
  1036.4 3.5 all-to-all-start.7
  1041.9 13.3 %all-to-all-done.7 = bf16[8,128,256]{1,2,0:T(8,128)(2,1)S(1)} async-done(((bf16[8,128,256]{1,2,0:T(8,128)(2,1)}), bf16[8,128,256]{1,2,0:T(8,128)(2,1)S(1)}, u32[]{:S(2)}, u32[]{:S(2)}) %all-to-all-start.7) | async-done | bytes 524320 | tf_op jit(solution)/shard_map/all_to_all | solution.py:183
  (842 shorter events, 564.5 us)
Async XLA Ops:
  0.6 22.4 %copy-start.4 = (bf16[128,2048]{1,0:T(8,128)(2,1)S(1)}, bf16[128,2048]{1,0:T(8,128)(2,1)}, u32[]{:S(2)}) copy-start(bf16[128,2048]{1,0:T(8,128)(2,1)} %param.13) | copy-start | bytes 1572868
  2.0 33.7 %collective-permute-start = (bf16[128,256]{0,1:T(8,128)(2,1)S(1)}, bf16[128,256]{0,1:T(8,128)(2,1)S(1)}, u32[]{:S(2)}, u32[]{:S(2)}) collective-permute-start(bf16[128,256]{0,1:T(8,128)(2,1)S(1)} %copy.440), channel_id=1, source_target_pairs={{0,1},{1,0},{2,3},{3,2},{4,5},{5,4},{6,7},{7,6},{8,9},{9,8},{10,11... | collective-permute-start | bytes 196616 | tf_op jit(solution)/shard_map/ppermute | solution.py:23
  2.6 36.8 %collective-permute-start.1 = (bf16[128,256]{0,1:T(8,128)(2,1)S(1)}, bf16[128,256]{0,1:T(8,128)(2,1)S(1)}, u32[]{:S(2)}, u32[]{:S(2)}) collective-permute-start(bf16[128,256]{0,1:T(8,128)(2,1)S(1)} %copy.441), channel_id=1, source_target_pairs={{0,2},{1,3},{2,0},{3,1},{4,6},{5,7},{6,4},{7,5},{8,10},{9,11},{10,... | collective-permute-start | bytes 196616 | tf_op jit(solution)/shard_map/ppermute | solution.py:23
  5.4 27.0 %copy-start.5 = (bf16[128,2048]{1,0:T(8,128)(2,1)S(1)}, bf16[128,2048]{1,0:T(8,128)(2,1)}, u32[]{:S(2)}) copy-start(bf16[128,2048]{1,0:T(8,128)(2,1)} %param.15) | copy-start | bytes 1572868
  5.4 34.1 %collective-permute-start.2 = (bf16[128,256]{0,1:T(8,128)(2,1)S(1)}, bf16[128,256]{0,1:T(8,128)(2,1)S(1)}, u32[]{:S(2)}, u32[]{:S(2)}) collective-permute-start(bf16[128,256]{0,1:T(8,128)(2,1)S(1)} %copy.442), channel_id=1, source_target_pairs={{0,3},{1,2},{2,1},{3,0},{4,7},{5,6},{6,5},{7,4},{8,11},{9,10},{10,... | collective-permute-start | bytes 196616 | tf_op jit(solution)/shard_map/ppermute | solution.py:23
  5.7 33.9 %collective-permute-start.3 = (bf16[128,256]{0,1:T(8,128)(2,1)S(1)}, bf16[128,256]{0,1:T(8,128)(2,1)S(1)}, u32[]{:S(2)}, u32[]{:S(2)}) collective-permute-start(bf16[128,256]{0,1:T(8,128)(2,1)S(1)} %copy.443), channel_id=1, source_target_pairs={{0,4},{1,5},{2,6},{3,7},{4,0},{5,1},{6,2},{7,3},{8,12},{9,13},{10,... | collective-permute-start | bytes 196616 | tf_op jit(solution)/shard_map/ppermute | solution.py:23
  8.6 45.5 %collective-permute-start.4 = (bf16[128,256]{0,1:T(8,128)(2,1)S(1)}, bf16[128,256]{0,1:T(8,128)(2,1)S(1)}, u32[]{:S(2)}, u32[]{:S(2)}) collective-permute-start(bf16[128,256]{0,1:T(8,128)(2,1)S(1)} %copy.444), channel_id=1, source_target_pairs={{0,5},{1,4},{2,7},{3,6},{4,1},{5,0},{6,3},{7,2},{8,13},{9,12},{10,... | collective-permute-start | bytes 196616 | tf_op jit(solution)/shard_map/ppermute | solution.py:23
  8.7 10.4 all-to-all-start.1
  16.0 17.4 %copy-start.6 = (bf16[128,2048]{1,0:T(8,128)(2,1)S(1)}, bf16[128,2048]{1,0:T(8,128)(2,1)}, u32[]{:S(2)}) copy-start(bf16[128,2048]{1,0:T(8,128)(2,1)} %param.18) | copy-start | bytes 1572868
  19.1 13.1 %copy-start.28 = (bf16[128,8,2]{0,2,1:T(2,128)(2,1)}, bf16[128,8,2]{0,2,1:T(2,128)(2,1)S(1)}, u32[]{:S(2)}) copy-start(bf16[128,8,2]{0,2,1:T(2,128)(2,1)S(1)} %all-to-all-done.1) | copy-start | bytes 12292
  19.1 8.7 all-to-all-start
  27.8 22.1 %all-to-all-start.3 = ((bf16[128,8,256]{0,2,1:T(8,128)(2,1)}), bf16[128,8,256]{0,2,1:T(8,128)(2,1)S(1)}, u32[]{:S(2)}, u32[]{:S(2)}) async-start(bf16[128,8,256]{0,2,1:T(8,128)(2,1)} %bitcast.20), calls=%async_computation.3 | async-start | bytes 1048576 | tf_op jit(solution)/shard_map/all_to_all | solution.py:164
  34.4 19.8 %copy-start.25 = (f32[1,2,8,128]{3,2,1,0:T(8,128)}, f32[1,2,8,128]{3,2,1,0:T(8,128)S(1)}, u32[]{:S(2)}) copy-start(f32[1,2,8,128]{3,2,1,0:T(8,128)S(1)} %divide_bitcast_fusion) | copy-start | bytes 24580
  35.6 18.5 %collective-permute-start.5 = (bf16[128,256]{0,1:T(8,128)(2,1)S(1)}, bf16[128,256]{0,1:T(8,128)(2,1)S(1)}, u32[]{:S(2)}, u32[]{:S(2)}) collective-permute-start(bf16[128,256]{0,1:T(8,128)(2,1)S(1)} %copy.445), channel_id=1, source_target_pairs={{0,6},{1,7},{2,4},{3,5},{4,2},{5,3},{6,0},{7,1},{8,14},{9,15},{10,... | collective-permute-start | bytes 196616 | tf_op jit(solution)/shard_map/ppermute | solution.py:23
  39.4 14.7 %collective-permute-start.6 = (bf16[128,256]{0,1:T(8,128)(2,1)S(1)}, bf16[128,256]{0,1:T(8,128)(2,1)S(1)}, u32[]{:S(2)}, u32[]{:S(2)}) collective-permute-start(bf16[128,256]{0,1:T(8,128)(2,1)S(1)} %copy.446), channel_id=1, source_target_pairs={{0,7},{1,6},{2,5},{3,4},{4,3},{5,2},{6,1},{7,0},{8,15},{9,14},{10,... | collective-permute-start | bytes 196616 | tf_op jit(solution)/shard_map/ppermute | solution.py:23
  49.9 19.5 %all-to-all-start.2 = ((bf16[128,8,256]{0,2,1:T(8,128)(2,1)}), bf16[128,8,256]{0,2,1:T(8,128)(2,1)}, u32[]{:S(2)}, u32[]{:S(2)}) async-start(bf16[128,8,256]{0,2,1:T(8,128)(2,1)} %bitcast.15), calls=%async_computation.2 | async-start | bytes 1048576 | tf_op jit(solution)/shard_map/all_to_all | solution.py:166
  69.4 21.1 %all-to-all-start.4 = ((bf16[128,8,256]{0,2,1:T(8,128)(2,1)}), bf16[128,8,256]{0,2,1:T(8,128)(2,1)}, u32[]{:S(2)}, u32[]{:S(2)}) async-start(bf16[128,8,256]{0,2,1:T(8,128)(2,1)} %bitcast.627), calls=%async_computation.4 | async-start | bytes 1048576 | tf_op jit(solution)/shard_map/all_to_all | solution.py:167
  103.5 27.1 %copy-start.1 = (f32[2,128]{1,0:T(2,128)}, f32[2,128]{1,0:T(2,128)S(1)}, u32[]{:S(2)}) copy-start(f32[2,128]{1,0:T(2,128)S(1)} %reduce_window_sum.46) | copy-start | bytes 3076 | tf_op jit(solution)/shard_map/jvp()/while
  109.4 30.3 %copy-start.7 = (f32[2,128]{1,0:T(2,128)S(1)}, f32[2,128]{1,0:T(2,128)}, u32[]{:S(2)}) copy-start(f32[2,128]{1,0:T(2,128)} %get-tuple-element.3083) | copy-start | bytes 3076 | tf_op jit(solution)/shard_map/jvp()/while
  146.0 27.2 %copy-start.1 = (f32[2,128]{1,0:T(2,128)}, f32[2,128]{1,0:T(2,128)S(1)}, u32[]{:S(2)}) copy-start(f32[2,128]{1,0:T(2,128)S(1)} %reduce_window_sum.46) | copy-start | bytes 3076 | tf_op jit(solution)/shard_map/jvp()/while
  151.9 31.2 %copy-start.7 = (f32[2,128]{1,0:T(2,128)S(1)}, f32[2,128]{1,0:T(2,128)}, u32[]{:S(2)}) copy-start(f32[2,128]{1,0:T(2,128)} %get-tuple-element.3083) | copy-start | bytes 3076 | tf_op jit(solution)/shard_map/jvp()/while
  173.2 10.7 %copy-start.9 = (f32[2,128]{1,0:T(2,128)S(1)}, f32[2,128]{1,0:T(2,128)}, u32[]{:S(2)}) copy-start(f32[2,128]{1,0:T(2,128)} %get-tuple-element.3084) | copy-start | bytes 3076 | tf_op jit(solution)/shard_map/jvp()/while
  176.4 10.0 copy-start.2
  189.5 27.2 %copy-start.1 = (f32[2,128]{1,0:T(2,128)}, f32[2,128]{1,0:T(2,128)S(1)}, u32[]{:S(2)}) copy-start(f32[2,128]{1,0:T(2,128)S(1)} %reduce_window_sum.46) | copy-start | bytes 3076 | tf_op jit(solution)/shard_map/jvp()/while
  195.4 31.2 %copy-start.7 = (f32[2,128]{1,0:T(2,128)S(1)}, f32[2,128]{1,0:T(2,128)}, u32[]{:S(2)}) copy-start(f32[2,128]{1,0:T(2,128)} %get-tuple-element.3083) | copy-start | bytes 3076 | tf_op jit(solution)/shard_map/jvp()/while
  216.6 10.7 %copy-start.9 = (f32[2,128]{1,0:T(2,128)S(1)}, f32[2,128]{1,0:T(2,128)}, u32[]{:S(2)}) copy-start(f32[2,128]{1,0:T(2,128)} %get-tuple-element.3084) | copy-start | bytes 3076 | tf_op jit(solution)/shard_map/jvp()/while
  232.9 27.2 %copy-start.1 = (f32[2,128]{1,0:T(2,128)}, f32[2,128]{1,0:T(2,128)S(1)}, u32[]{:S(2)}) copy-start(f32[2,128]{1,0:T(2,128)S(1)} %reduce_window_sum.46) | copy-start | bytes 3076 | tf_op jit(solution)/shard_map/jvp()/while
  238.8 31.2 %copy-start.7 = (f32[2,128]{1,0:T(2,128)S(1)}, f32[2,128]{1,0:T(2,128)}, u32[]{:S(2)}) copy-start(f32[2,128]{1,0:T(2,128)} %get-tuple-element.3083) | copy-start | bytes 3076 | tf_op jit(solution)/shard_map/jvp()/while
  260.1 10.7 %copy-start.9 = (f32[2,128]{1,0:T(2,128)S(1)}, f32[2,128]{1,0:T(2,128)}, u32[]{:S(2)}) copy-start(f32[2,128]{1,0:T(2,128)} %get-tuple-element.3084) | copy-start | bytes 3076 | tf_op jit(solution)/shard_map/jvp()/while
  276.3 27.1 %copy-start.1 = (f32[2,128]{1,0:T(2,128)}, f32[2,128]{1,0:T(2,128)S(1)}, u32[]{:S(2)}) copy-start(f32[2,128]{1,0:T(2,128)S(1)} %reduce_window_sum.46) | copy-start | bytes 3076 | tf_op jit(solution)/shard_map/jvp()/while
  282.3 31.2 %copy-start.7 = (f32[2,128]{1,0:T(2,128)S(1)}, f32[2,128]{1,0:T(2,128)}, u32[]{:S(2)}) copy-start(f32[2,128]{1,0:T(2,128)} %get-tuple-element.3083) | copy-start | bytes 3076 | tf_op jit(solution)/shard_map/jvp()/while
  303.5 10.7 %copy-start.9 = (f32[2,128]{1,0:T(2,128)S(1)}, f32[2,128]{1,0:T(2,128)}, u32[]{:S(2)}) copy-start(f32[2,128]{1,0:T(2,128)} %get-tuple-element.3084) | copy-start | bytes 3076 | tf_op jit(solution)/shard_map/jvp()/while
  319.8 27.1 %copy-start.1 = (f32[2,128]{1,0:T(2,128)}, f32[2,128]{1,0:T(2,128)S(1)}, u32[]{:S(2)}) copy-start(f32[2,128]{1,0:T(2,128)S(1)} %reduce_window_sum.46) | copy-start | bytes 3076 | tf_op jit(solution)/shard_map/jvp()/while
  325.7 31.2 %copy-start.7 = (f32[2,128]{1,0:T(2,128)S(1)}, f32[2,128]{1,0:T(2,128)}, u32[]{:S(2)}) copy-start(f32[2,128]{1,0:T(2,128)} %get-tuple-element.3083) | copy-start | bytes 3076 | tf_op jit(solution)/shard_map/jvp()/while
  346.9 10.7 %copy-start.9 = (f32[2,128]{1,0:T(2,128)S(1)}, f32[2,128]{1,0:T(2,128)}, u32[]{:S(2)}) copy-start(f32[2,128]{1,0:T(2,128)} %get-tuple-element.3084) | copy-start | bytes 3076 | tf_op jit(solution)/shard_map/jvp()/while
  363.2 27.1 %copy-start.1 = (f32[2,128]{1,0:T(2,128)}, f32[2,128]{1,0:T(2,128)S(1)}, u32[]{:S(2)}) copy-start(f32[2,128]{1,0:T(2,128)S(1)} %reduce_window_sum.46) | copy-start | bytes 3076 | tf_op jit(solution)/shard_map/jvp()/while
  369.2 31.2 %copy-start.7 = (f32[2,128]{1,0:T(2,128)S(1)}, f32[2,128]{1,0:T(2,128)}, u32[]{:S(2)}) copy-start(f32[2,128]{1,0:T(2,128)} %get-tuple-element.3083) | copy-start | bytes 3076 | tf_op jit(solution)/shard_map/jvp()/while
  390.4 10.7 %copy-start.9 = (f32[2,128]{1,0:T(2,128)S(1)}, f32[2,128]{1,0:T(2,128)}, u32[]{:S(2)}) copy-start(f32[2,128]{1,0:T(2,128)} %get-tuple-element.3084) | copy-start | bytes 3076 | tf_op jit(solution)/shard_map/jvp()/while
  406.7 27.2 %copy-start.1 = (f32[2,128]{1,0:T(2,128)}, f32[2,128]{1,0:T(2,128)S(1)}, u32[]{:S(2)}) copy-start(f32[2,128]{1,0:T(2,128)S(1)} %reduce_window_sum.46) | copy-start | bytes 3076 | tf_op jit(solution)/shard_map/jvp()/while
  412.6 31.1 %copy-start.7 = (f32[2,128]{1,0:T(2,128)S(1)}, f32[2,128]{1,0:T(2,128)}, u32[]{:S(2)}) copy-start(f32[2,128]{1,0:T(2,128)} %get-tuple-element.3083) | copy-start | bytes 3076 | tf_op jit(solution)/shard_map/jvp()/while
  433.8 10.7 %copy-start.9 = (f32[2,128]{1,0:T(2,128)S(1)}, f32[2,128]{1,0:T(2,128)}, u32[]{:S(2)}) copy-start(f32[2,128]{1,0:T(2,128)} %get-tuple-element.3084) | copy-start | bytes 3076 | tf_op jit(solution)/shard_map/jvp()/while
  977.4 15.9 %copy-start.20 = (f32[2,1024]{1,0:T(2,128)S(1)}, f32[2,1024]{1,0:T(2,128)}, u32[]{:S(2)}) copy-start(f32[2,1024]{1,0:T(2,128)} %copy-done.19) | copy-start | bytes 24580
  979.8 10.3 all-to-all-start.8
  990.1 8.7 all-to-all-start.9
  998.8 18.8 %all-to-all-start.6 = ((bf16[8,128,256]{1,2,0:T(8,128)(2,1)}), bf16[8,128,256]{1,2,0:T(8,128)(2,1)S(1)}, u32[]{:S(2)}, u32[]{:S(2)}) async-start(bf16[8,128,256]{1,2,0:T(8,128)(2,1)} %copy.406), calls=%async_computation.6 | async-start | bytes 1048576 | tf_op jit(solution)/shard_map/all_to_all | solution.py:182
  1004.4 16.7 %copy-start.3 = (bf16[8,2,128,128]{3,2,0,1:T(8,128)(2,1)S(1)}, bf16[8,2,128,128]{3,2,0,1:T(8,128)(2,1)}, u32[]{:S(2)}) copy-start(bf16[8,2,128,128]{3,2,0,1:T(8,128)(2,1)} %get-tuple-element.1507) | copy-start | bytes 1572868
  1017.6 18.8 %all-to-all-start.5 = ((bf16[8,128,256]{1,2,0:T(8,128)(2,1)}), bf16[8,128,256]{1,2,0:T(8,128)(2,1)S(1)}, u32[]{:S(2)}, u32[]{:S(2)}) async-start(bf16[8,128,256]{1,2,0:T(8,128)(2,1)} %copy.402), calls=%async_computation.5 | async-start | bytes 1048576 | tf_op jit(solution)/shard_map/all_to_all | solution.py:181
  1036.4 18.8 %all-to-all-start.7 = ((bf16[8,128,256]{1,2,0:T(8,128)(2,1)}), bf16[8,128,256]{1,2,0:T(8,128)(2,1)S(1)}, u32[]{:S(2)}, u32[]{:S(2)}) async-start(bf16[8,128,256]{1,2,0:T(8,128)(2,1)} %copy.409), calls=%async_computation.7 | async-start | bytes 1048576 | tf_op jit(solution)/shard_map/all_to_all | solution.py:183
  (78 other events, 367.4 us)
